TPU v7x, 32 devices: a whole 2x2x4 slice. The times are simulated.
32 devices in a mesh: grp: 2 (over x), tpl: 16 (over z, y, core).
Axes of the slice: x: 2, y: 2, z: 4, core: 2. Of those that a mesh axis runs over, the one named last changes fastest.
Arguments:
- strain_slots: bfloat16 [32, 3, 2, 262144], P(('grp', 'tpl')), parts along dimension 0, may hold values from -6 to 6
- templates: bfloat16 [32, 2, 262144], P(None, None, 'tpl'), may hold values from -6 to 6
- cutoffs: int32 [32], replicated, may hold values from 32768 to 262144
- lists: int32 [16, 2], replicated, may hold values from 0 to 31, as said below
- owner: int32 [2], P('grp'), parts along dimension 0, may hold values from 0 to 15
- slides: int32 [6], P('grp'), parts along dimension 0, may hold values from 0 to 262143
Outputs:
- peaks: float32 [64], P(('grp', 'tpl')), parts along dimension 0
- norms: float32 [64], P(('grp', 'tpl')), parts along dimension 0
There are 2 independent parts, one for each index of `grp`. A program takes and returns all parts, laid end to end along the dimension named above; an argument that names none is the same for every part. Nothing has to cross between parts.
Inputs may be any that keep to these rules, and one draw needn't show every extreme that they name: Every template appears once in lists; list positions in row-major order run through the templates by falling cutoffs. One template has cutoff 262144, one has 32768.
All inputs are finite; a program needn't handle non-finite values.
Results may differ from a plain program's by a relative error of at most 0.0021.
Values may be sent and summed in bfloat16 or wider, within the bound.
A program may use at most 128 MiB of HBM per device.

v0:
```python
import jax
import jax.numpy as jnp
from jax import lax
from jax.sharding import PartitionSpec as P

DET = 3
ROWS = 512
COLS = 512
BLOCK_ROWS = 64
two_pi = 6.283185307179586
eps_norm = 1e-06


def spread(block, axis, owner):
    block = jnp.where(lax.axis_index(axis) == owner, block, jnp.zeros_like(block))
    return lax.psum(block, axis)


def turn_table(left_ids, right_ids, period):
    product_idx = left_ids[:, None] * right_ids[None, :] % period
    angles = product_idx.astype(jnp.float32) * (two_pi / period)
    return (jnp.cos(angles), jnp.sin(angles))


def slide_phases(slides):
    total = ROWS * COLS
    bin_ids = jnp.arange(total, dtype=jnp.int32)
    row_ids = bin_ids // COLS
    col_ids = bin_ids % COLS
    stride = COLS * slides % total
    turns = (
        row_ids[None, :] * stride[:, None] % total + col_ids[None, :] * slides[:, None] % total
    ) % total
    angles = turns.astype(jnp.float32) * (two_pi / total)
    return (jnp.cos(angles), jnp.sin(angles))


def body(strain_slots, templates, cutoffs, lists, owner, slides):
    total = ROWS * COLS
    block_count_all = ROWS // BLOCK_ROWS
    devices = lax.axis_size("tpl")
    own_index = lax.axis_index("tpl")
    per_device = lists.shape[1]
    strain = spread(strain_slots[0], "tpl", owner[0])
    flat_list = lists.reshape(-1)
    device_ids = jnp.arange(devices, dtype=jnp.int32)[:, None]
    slot_ids = jnp.arange(per_device, dtype=jnp.int32)[None, :]
    positions = device_ids * per_device + slot_ids
    chosen = flat_list[positions]
    picked = templates[chosen.reshape(-1)]
    picked = picked.reshape(devices, per_device, 2, templates.shape[2])
    arrived = lax.all_to_all(picked, "tpl", split_axis=0, concat_axis=3, tiled=True)[0]
    own_ids = lax.dynamic_index_in_dim(chosen, own_index, 0, keepdims=False)
    cutoff_bins = cutoffs[own_ids]
    row_ids = jnp.arange(ROWS, dtype=jnp.int32)
    col_ids = jnp.arange(COLS, dtype=jnp.int32)
    row_cos, row_sin = turn_table(row_ids, row_ids, ROWS)
    cos_blocks = row_cos.reshape(ROWS, block_count_all, BLOCK_ROWS).transpose(1, 0, 2)
    sin_blocks = row_sin.reshape(ROWS, block_count_all, BLOCK_ROWS).transpose(1, 0, 2)
    row_blocks = jnp.concatenate(
        [
            jnp.concatenate([cos_blocks, -sin_blocks], 2),
            jnp.concatenate([sin_blocks, cos_blocks], 2),
        ],
        1,
    ).astype(jnp.bfloat16)
    twiddle_cos, twiddle_sin = turn_table(row_ids, col_ids, total)
    col_cos, col_sin = turn_table(col_ids, col_ids, COLS)
    col_table = jnp.concatenate(
        [jnp.concatenate([col_cos, col_sin], 1), jnp.concatenate([-col_sin, col_cos], 1)], 0
    ).astype(jnp.bfloat16)
    phase_cos, phase_sin = slide_phases(slides)
    data_re = strain[:, 0].astype(jnp.float32)
    data_im = strain[:, 1].astype(jnp.float32)

    def filter_one(packed):
        waveform, cutoff = packed
        inside = jnp.arange(total, dtype=jnp.int32) < cutoff
        wave_re = waveform[0].astype(jnp.float32)
        wave_im = waveform[1].astype(jnp.float32)
        real_part = data_re * wave_re + data_im * wave_im
        imag_part = data_im * wave_re - data_re * wave_im
        prod_re = jnp.where(inside, real_part * phase_cos - imag_part * phase_sin, 0.0)
        prod_im = jnp.where(inside, real_part * phase_sin + imag_part * phase_cos, 0.0)
        stacked = jnp.concatenate(
            [
                prod_re.reshape(DET, block_count_all, BLOCK_ROWS, COLS),
                prod_im.reshape(DET, block_count_all, BLOCK_ROWS, COLS),
            ],
            2,
        ).astype(jnp.bfloat16)
        section_one = jnp.einsum(
            "bai,dbic->dac", row_blocks, stacked, preferred_element_type=jnp.float32
        )
        first_re = section_one[:, :ROWS]
        first_im = section_one[:, ROWS:]
        twisted = jnp.concatenate(
            [
                first_re * twiddle_cos - first_im * twiddle_sin,
                first_re * twiddle_sin + first_im * twiddle_cos,
            ],
            2,
        ).astype(jnp.bfloat16)
        series = jnp.einsum("dab,bc->dac", twisted, col_table, preferred_element_type=jnp.float32)
        squares = jnp.sum(series * series, axis=0)
        power_sum = squares[:, :COLS] + squares[:, COLS:]
        sigmasq = jnp.sum(jnp.where(inside, wave_re * wave_re + wave_im * wave_im, 0.0))
        return (jnp.max(power_sum) / (2.0 * (sigmasq + eps_norm)), sigmasq / total)

    peaks, norms = lax.map(filter_one, (arrived, cutoff_bins))
    return (peaks, norms)


def solution(mesh):
    in_specs = (
        P(("grp", "tpl"), None, None, None),
        P(None, None, "tpl"),
        P(),
        P(),
        P("grp"),
        P("grp"),
    )
    out_specs = (P(("grp", "tpl")), P(("grp", "tpl")))
    return jax.shard_map(body, mesh=mesh, in_specs=in_specs, out_specs=out_specs, check_vma=False)
```

profile of v0, /device:TPU:0, one launch (start us, length us, event | category | flops | bytes accessed | tf_op | source)
XLA Modules:
  0.0 458.4 jit_solution(1903081071991389454)
XLA Ops:
  8.0 10.3 %fusion.41 = bf16[3,2,262144]{2,0,1:T(4,128)(2,1)} fusion(bf16[1,3,2,262144]{3,2,1,0:T(2,128)(2,1)} %param.8, pred[]{:T(512)S(6)} %eq.15), kind=kLoop, calls=%fused_computation.69 | loop fusion | flops 1572864 | bytes 6291457 | tf_op jit(solution)/shard_map/jit(_where)/select_n | solution.py:15
  19.9 6.1 %gather_fusion.2 = bf16[32,2,16384]{2,1,0:T(2,128)(2,1)} fusion(bf16[32,2,16384]{2,1,0:T(2,128)(2,1)S(1)} %copy-done, s32[1024]{0:T(1024)S(1)} %pad_clamp_fusion), kind=kCustom, calls=%fused_computation.2 | custom fusion | bytes 4194432 | tf_op jit(solution)/shard_map/gather | solution.py:50
  26.0 7.8 %all-to-all-start = ((bf16[16,2,2,16384]{3,2,1,0:T(2,128)(2,1)}), bf16[16,2,2,16384]{3,2,1,0:T(2,128)(2,1)}, u32[]{:S(2)}, u32[]{:S(2)}) async-start(bf16[16,2,2,16384]{3,2,1,0:T(2,128)(2,1)} %bitcast.96), calls=%async_computation | async-start | bytes 4194304 | tf_op jit(solution)/shard_map/all_to_all | solution.py:52
  33.8 1.5 fusion.49
  36.1 4.0 fusion.66
  40.1 4.3 negate_convert_fusion.1
  44.4 8.7 %negate_convert_fusion = (bf16[8,512,64]{2,1,0:T(8,128)(2,1)S(1)}, bf16[8,512,64]{2,1,0:T(8,128)(2,1)S(1)}, bf16[8,512,64]{2,1,0:T(8,128)(2,1)S(1)}) fusion(s32[8,64]{1,0:T(8,128)S(1)} %multiply_add_fusion.2), kind=kLoop, calls=%fused_computation.82 | loop fusion | flops 4718592 | bytes 1574912 | tf_op jit(solution)/shard_map/convert.19
  53.1 2.5 maximum_maximum_fusion
  55.6 1.6 maximum_maximum_fusion.1
  57.2 115.2 %all-reduce.2.cloned.1.call-done = bf16[3,2,262144]{2,0,1:T(4,128)(2,1)} async-done(((bf16[3,2,262144]{2,0,1:T(4,128)(2,1)}), bf16[3,2,262144]{2,0,1:T(4,128)(2,1)}) %all-reduce.2.cloned.1.call-update) | async-done | bytes 3145744 | tf_op jit(solution)/shard_map/psum | solution.py:16
  172.4 5.0 %fusion.45 = (f32[3,262144]{1,0:T(4,128)}, f32[3,262144]{1,0:T(4,128)}) fusion(bf16[3,2,262144]{2,0,1:T(4,128)(2,1)} %all-reduce.2.cloned.1.call-done), kind=kLoop, calls=%fused_computation.77 | loop fusion | flops 1572864 | bytes 9437184 | tf_op jit(solution)/shard_map/convert_element_type | solution.py:74
  177.4 2.7 copy.68
  180.1 2.5 squeeze.23
  182.7 267.2 %while.15 = (s32[]{:T(128)}, f32[2]{0:T(128)S(1)}, f32[2]{0:T(128)S(1)}, s32[2]{0:T(128)S(1)}, f32[3,262144]{1,0:T(4,128)}, /*index=5*/bf16[2,2,262144]{2,1,0:T(...) while((s32[]{:T(128)}, f32[2]{0:T(128)S(1)}, ...), condition=%wide.region_5.6_spmd.clone.clone.clone, body=%wide.region_1.5_spmd.clone.clone.clone.sunk | while | flops 6514016256 | bytes 146276784 | solution.py:110
  183.0 16.5 %fusion.84 = (f32[262144]{0:T(1024)}, f32[262144]{0:T(1024)S(1)}, f32[1,1,262144]{2,1,0:T(1,128)}) fusion(bf16[2,2,262144]{2,1,0:T(2,128)(2,1)} %get-tuple-element.387, s32[]{:T(128)} %get-tuple-element.363, s32[]{:T(128)S(6)} %add.959), kind=kLoop, calls=%fused_computation.62.clone.1 | loop fusion | flops 1310720 | bytes 4194312 | tf_op jit(solution)/shard_map/while/body/eval_jaxpr/convert_element_type | solution.py:79
  200.3 1.4 reshape.324
  201.7 1.9 copy.97
  205.2 42.2 %fusion.83 = (f32[3,262144]{1,0:T(4,128)S(1)}, f32[3,262144]{1,0:T(4,128)}) fusion(s32[3]{0:T(128)S(1)} %get-tuple-element.393, s32[262144]{0:T(1024)} %get-tuple-element.394, s32[3]{0:T(128)S(1)} %get-tuple-element.391, s32[262144]{0:T(1024)} %get-tuple-element.392), kind=kLoop, calls=%fused_computation.43.clone.1 | loop fusion | flops 29884416 | bytes 8388632 | tf_op jit(solution)/shard_map/sin | solution.py:35
  247.5 2.7 copy.88
  250.2 5.8 %copy.89 = f32[3,8,64,512]{2,3,1,0:T(8,128)} copy(f32[3,8,64,512]{3,2,1,0:T(8,128)} %bitcast.89) | data formatting | bytes 6291456 | tf_op jit(solution)/shard_map/reshape.31
  255.9 4.8 %copy.90 = f32[1,3,512,512]{3,2,1,0:T(8,128)} copy(f32[1,3,512,512]{3,1,2,0:T(4,128)} %bitcast.87) | data formatting | bytes 6291456 | tf_op jit(solution)/shard_map/while
  260.8 5.8 %copy.91 = f32[3,8,64,512]{2,3,1,0:T(8,128)} copy(f32[3,8,64,512]{3,2,1,0:T(8,128)} %bitcast.90) | data formatting | bytes 6291456 | tf_op jit(solution)/shard_map/reshape.26
  266.5 4.9 %copy.92 = f32[1,3,512,512]{3,2,1,0:T(8,128)} copy(f32[1,3,512,512]{3,1,2,0:T(4,128)} %bitcast.93) | data formatting | bytes 6291456 | tf_op jit(solution)/shard_map/while
  271.4 5.8 %copy.93 = f32[3,8,64,512]{2,3,1,0:T(8,128)} copy(f32[3,8,64,512]{3,2,1,0:T(8,128)} %bitcast.91) | data formatting | bytes 6291456 | tf_op jit(solution)/shard_map/reshape.23
  277.2 4.8 %copy.95 = f32[1,3,512,512]{3,2,1,0:T(8,128)} copy(f32[1,3,512,512]{3,1,2,0:T(4,128)} %bitcast.94) | data formatting | bytes 6291456 | tf_op jit(solution)/shard_map/while
  282.0 5.8 %copy.96 = f32[3,8,64,512]{2,3,1,0:T(8,128)} copy(f32[3,8,64,512]{3,2,1,0:T(8,128)} %bitcast.92) | data formatting | bytes 6291456 | tf_op jit(solution)/shard_map/reshape.20
  287.8 10.7 %select_convert_fusion.3 = (bf16[3,8,64,512]{2,3,1,0:T(8,128)(2,1)S(1)}, bf16[3,8,64,512]{2,3,1,0:T(8,128)(2,1)S(1)}) fusion(f32[3,8,64,512]{2,3,1,0:T(8,128)} %copy.89, f32[3,8,64,512]{2,3,1,0:T(8,128)} %copy.91, pred[8,64,512]{1,2,0:T(8,128)(4,1)S(1)} %add_compare_fusion.2, f32[3,8,64,512]{2,3,1,0:T(8,128)} %copy.93, f32[8,64,512]{1,2,0:T(8,128)S(1)} %copy.94, ...), kind=kLoop, calls=%fused_computation.22.clone.1 | loop fusion | flops 12582912 | bytes 18087936 | tf_op jit(solution)/shard_map/convert.4
  298.5 3.6 fusion.85
  302.1 4.1 fusion.86
  307.8 3.9 multiply_reduce_fusion.2
  312.6 1.6 select_reduce_fusion.2
  316.3 16.6 %fusion.84 = (f32[262144]{0:T(1024)}, f32[262144]{0:T(1024)S(1)}, f32[1,1,262144]{2,1,0:T(1,128)}) fusion(bf16[2,2,262144]{2,1,0:T(2,128)(2,1)} %get-tuple-element.387, s32[]{:T(128)} %get-tuple-element.363, s32[]{:T(128)S(6)} %add.959), kind=kLoop, calls=%fused_computation.62.clone.1 | loop fusion | flops 1310720 | bytes 4194312 | tf_op jit(solution)/shard_map/while/body/eval_jaxpr/convert_element_type | solution.py:79
  333.8 1.4 reshape.324
  335.2 1.9 copy.97
  338.7 42.2 %fusion.83 = (f32[3,262144]{1,0:T(4,128)S(1)}, f32[3,262144]{1,0:T(4,128)}) fusion(s32[3]{0:T(128)S(1)} %get-tuple-element.393, s32[262144]{0:T(1024)} %get-tuple-element.394, s32[3]{0:T(128)S(1)} %get-tuple-element.391, s32[262144]{0:T(1024)} %get-tuple-element.392), kind=kLoop, calls=%fused_computation.43.clone.1 | loop fusion | flops 29884416 | bytes 8388632 | tf_op jit(solution)/shard_map/sin | solution.py:35
  380.9 2.7 copy.88
  383.6 5.8 %copy.89 = f32[3,8,64,512]{2,3,1,0:T(8,128)} copy(f32[3,8,64,512]{3,2,1,0:T(8,128)} %bitcast.89) | data formatting | bytes 6291456 | tf_op jit(solution)/shard_map/reshape.31
  389.4 4.8 %copy.90 = f32[1,3,512,512]{3,2,1,0:T(8,128)} copy(f32[1,3,512,512]{3,1,2,0:T(4,128)} %bitcast.87) | data formatting | bytes 6291456 | tf_op jit(solution)/shard_map/while
  394.2 5.8 %copy.91 = f32[3,8,64,512]{2,3,1,0:T(8,128)} copy(f32[3,8,64,512]{3,2,1,0:T(8,128)} %bitcast.90) | data formatting | bytes 6291456 | tf_op jit(solution)/shard_map/reshape.26
  400.0 4.9 %copy.92 = f32[1,3,512,512]{3,2,1,0:T(8,128)} copy(f32[1,3,512,512]{3,1,2,0:T(4,128)} %bitcast.93) | data formatting | bytes 6291456 | tf_op jit(solution)/shard_map/while
  404.9 5.8 %copy.93 = f32[3,8,64,512]{2,3,1,0:T(8,128)} copy(f32[3,8,64,512]{3,2,1,0:T(8,128)} %bitcast.91) | data formatting | bytes 6291456 | tf_op jit(solution)/shard_map/reshape.23
  410.6 4.8 %copy.95 = f32[1,3,512,512]{3,2,1,0:T(8,128)} copy(f32[1,3,512,512]{3,1,2,0:T(4,128)} %bitcast.94) | data formatting | bytes 6291456 | tf_op jit(solution)/shard_map/while
  415.5 5.8 %copy.96 = f32[3,8,64,512]{2,3,1,0:T(8,128)} copy(f32[3,8,64,512]{3,2,1,0:T(8,128)} %bitcast.92) | data formatting | bytes 6291456 | tf_op jit(solution)/shard_map/reshape.20
  421.2 10.7 %select_convert_fusion.3 = (bf16[3,8,64,512]{2,3,1,0:T(8,128)(2,1)S(1)}, bf16[3,8,64,512]{2,3,1,0:T(8,128)(2,1)S(1)}) fusion(f32[3,8,64,512]{2,3,1,0:T(8,128)} %copy.89, f32[3,8,64,512]{2,3,1,0:T(8,128)} %copy.91, pred[8,64,512]{1,2,0:T(8,128)(4,1)S(1)} %add_compare_fusion.2, f32[3,8,64,512]{2,3,1,0:T(8,128)} %copy.93, f32[8,64,512]{1,2,0:T(8,128)S(1)} %copy.94, ...), kind=kLoop, calls=%fused_computation.22.clone.1 | loop fusion | flops 12582912 | bytes 18087936 | tf_op jit(solution)/shard_map/convert.4
  432.0 3.6 fusion.85
  435.6 4.1 fusion.86
  441.3 3.9 multiply_reduce_fusion.2
  446.1 1.6 select_reduce_fusion.2
  (62 shorter events, 14.0 us)
Async XLA Ops:
  7.2 12.7 %copy-start = (bf16[32,2,16384]{2,1,0:T(2,128)(2,1)S(1)}, bf16[32,2,16384]{2,1,0:T(2,128)(2,1)}, u32[]{:S(2)}) copy-start(bf16[32,2,16384]{2,1,0:T(2,128)(2,1)} %param.9) | copy-start | bytes 6291460
  7.2 165.2 %all-reduce.2.cloned.1.call-start = ((), (), s32[]{:S(2)}) async-start(), calls=%async_computation.1 | async-start | bytes 8388608 | tf_op jit(solution)/shard_map/psum | solution.py:16
  18.3 0.7 copy-start.7
  26.0 9.4 %copy-start.2 = (s32[32]{0:T(128)S(1)}, s32[32]{0:T(128)}, u32[]{:S(2)}) copy-start(s32[32]{0:T(128)} %param.10) | copy-start | bytes 388
  26.0 151.3 %all-to-all-start = ((bf16[16,2,2,16384]{3,2,1,0:T(2,128)(2,1)}), bf16[16,2,2,16384]{3,2,1,0:T(2,128)(2,1)}, u32[]{:S(2)}, u32[]{:S(2)}) async-start(bf16[16,2,2,16384]{3,2,1,0:T(2,128)(2,1)} %bitcast.96), calls=%async_computation | async-start | bytes 4194304 | tf_op jit(solution)/shard_map/all_to_all | solution.py:52
  55.6 1.6 copy-start.6
  287.8 10.7 %copy-start.5 = (bf16[8,1024,128]{2,1,0:T(8,128)(2,1)S(1)}, bf16[8,1024,128]{2,1,0:T(8,128)(2,1)}, u32[]{:S(2)}) copy-start(bf16[8,1024,128]{2,1,0:T(8,128)(2,1)} %get-tuple-element.389) | copy-start | bytes 6291460 | tf_op jit(solution)/shard_map/while
  306.2 1.6 copy-start.4
  307.8 4.8 %copy-start.3 = (f32[1,1,262144]{2,1,0:T(1,128)S(1)}, f32[1,1,262144]{2,1,0:T(1,128)}, u32[]{:S(2)}) copy-start(f32[1,1,262144]{2,1,0:T(1,128)} %get-tuple-element.343) | copy-start | bytes 3145732 | tf_op jit(solution)/shard_map/while
  421.2 10.7 %copy-start.5 = (bf16[8,1024,128]{2,1,0:T(8,128)(2,1)S(1)}, bf16[8,1024,128]{2,1,0:T(8,128)(2,1)}, u32[]{:S(2)}) copy-start(bf16[8,1024,128]{2,1,0:T(8,128)(2,1)} %get-tuple-element.389) | copy-start | bytes 6291460 | tf_op jit(solution)/shard_map/while
  439.7 1.6 copy-start.4
  441.3 4.8 %copy-start.3 = (f32[1,1,262144]{2,1,0:T(1,128)S(1)}, f32[1,1,262144]{2,1,0:T(1,128)}, u32[]{:S(2)}) copy-start(f32[1,1,262144]{2,1,0:T(1,128)} %get-tuple-element.343) | copy-start | bytes 3145732 | tf_op jit(solution)/shard_map/while
  449.8 0.5 copy-start.8
  449.8 0.5 copy-start.9
  449.8 1.6 copy-start.1
Sparse Core Ops, SparseCore 0:
  18.5 153.8 all-reduce.1
where the time goes:
time: 464 us; the launch traced here: 458 us
  other arithmetic  195 us (42%)
  waiting for transfers between devices  115 us (25%)
  local copies, waits for them, and re-layouts  106 us (23%)
  matrix products  15.1 us (3%)
  between operations  15.1 us (3%)
  starting transfers between devices  7.82 us (2%)
    psum x1, waiting for transfers between devices, spread(): return lax.psum(block, axis)  115 us
    sin x2, other arithmetic, slide_phases(): return (jnp.cos(angles), jnp.sin(angles))  84.5 us
    another operation x8, local copies, waits for them, and re-layouts  46.1 us
    another operation x9, other arithmetic  40.9 us
    while x20, local copies, waits for them, and re-layouts  35.1 us
    convert_element_type x2, other arithmetic, filter_one(): wave_re = waveform[0].astype(jnp.float32)  33.1 us
    select_n x1, other arithmetic, spread(): jnp.where(lax.axis_index(axis) == owner, block, jnp.zeros_like(block))  10.3 us
  transfers between devices with their start and end apart: 2, of which 1 were waited for; matrix products, arithmetic and copies ran while one was open for 8% of the time, Pallas kernels for 0%

commit v1 on v0

--- a/solution.py
+++ b/solution.py
@@ -13,7 +13,7 @@
 
 def spread(block, axis, owner):
     block = jnp.where(lax.axis_index(axis) == owner, block, jnp.zeros_like(block))
-    return lax.psum(block, axis)
+    return jnp.sum(lax.all_gather(block, axis), axis=0)
 
 
 def turn_table(left_ids, right_ids, period):

time: 464 us -> 662 us (1.43)
  the two profiles are of different devices: /device:TPU:0 before, /device:TPU:9 now
where the time goes in v1:
time: 662 us; the launch traced here: 658 us
  waiting for transfers between devices  251 us (38%)
  other arithmetic  240 us (36%)
  local copies, waits for them, and re-layouts  114 us (17%)
  loops' own time  16.1 us (2%)
  matrix products  15.1 us (2%)
  between operations  15.1 us (2%)
  starting transfers between devices  6.94 us (1%)
    all_gather x1, waiting for transfers between devices, spread(): return jnp.sum(lax.all_gather(block, axis), axis=0)  204 us
    sin x2, other arithmetic, slide_phases(): return (jnp.cos(angles), jnp.sin(angles))  84.5 us
    reduce_sum x1, other arithmetic, spread(): return jnp.sum(lax.all_gather(block, axis), axis=0)  48.8 us
    all_to_all x1, waiting for transfers between devices, body(): lax.all_to_all(picked, 'tpl', split_axis=0, concat_axis=3, tiled=True)[0]  46.6 us
    another operation x8, local copies, waits for them, and re-layouts  46.1 us
    another operation x9, other arithmetic  40.9 us
    while x20, local copies, waits for them, and re-layouts  35.1 us
    convert_element_type x2, other arithmetic, filter_one(): wave_re = waveform[0].astype(jnp.float32)  33.1 us
  transfers between devices with their start and end apart: 2, of which 2 were waited for; matrix products, arithmetic and copies ran while one was open for 5% of the time, Pallas kernels for 0%

profile of v1, /device:TPU:9, one launch (start us, length us, event | category | flops | bytes accessed | tf_op | source)
XLA Modules:
  0.0 657.6 jit_solution(1576149197317656751)
XLA Ops:
  8.0 4.2 broadcast_select_fusion
  13.8 6.2 gather_fusion.2
  19.9 6.9 %all-to-all-start = ((bf16[16,2,2,16384]{3,2,1,0:T(2,128)(2,1)}), bf16[16,2,2,16384]{3,2,1,0:T(2,128)(2,1)}, u32[]{:S(2)}, u32[]{:S(2)}) async-start(bf16[16,2,2,16384]{3,2,1,0:T(2,128)(2,1)} %bitcast.88), calls=%async_computation | async-start | bytes 4194304 | tf_op jit(solution)/shard_map/all_to_all | solution.py:52
  27.0 4.0 fusion.63
  30.9 4.3 negate_convert_fusion.1
  35.3 8.7 %negate_convert_fusion = (bf16[8,512,64]{2,1,0:T(8,128)(2,1)S(1)}, bf16[8,512,64]{2,1,0:T(8,128)(2,1)S(1)}, bf16[8,512,64]{2,1,0:T(8,128)(2,1)S(1)}) fusion(s32[8,64]{1,0:T(8,128)S(1)} %multiply_add_fusion.2), kind=kLoop, calls=%fused_computation.81 | loop fusion | flops 4718592 | bytes 1574912 | tf_op jit(solution)/shard_map/convert.20
  44.0 2.5 maximum_maximum_fusion
  46.5 1.6 maximum_maximum_fusion.1
  50.2 46.6 %all-to-all-done = bf16[16,2,2,16384]{3,2,1,0:T(2,128)(2,1)} async-done(((bf16[16,2,2,16384]{3,2,1,0:T(2,128)(2,1)}), bf16[16,2,2,16384]{3,2,1,0:T(2,128)(2,1)}, u32[]{:S(2)}, u32[]{:S(2)}) %all-to-all-start) | async-done | bytes 2097184 | tf_op jit(solution)/shard_map/all_to_all | solution.py:52
  96.8 2.7 copy.63
  99.5 2.5 squeeze.23
  102.1 204.0 %all-gather.2.cloned.1.call-done = bf16[16,3,2,262144]{3,2,1,0:T(2,128)(2,1)} async-done(((bf16[1,3,2,262144]{3,2,1,0:T(2,128)(2,1)}), bf16[16,3,2,262144]{3,2,1,0:T(2,128)(2,1)}) %all-gather.2.cloned.1.call-update) | async-done | bytes 50331664 | tf_op jit(solution)/shard_map/all_gather | solution.py:16
  306.1 48.8 %reduce_sum.30 = bf16[3,2,262144]{2,1,0:T(2,128)(2,1)} reduce(bf16[16,3,2,262144]{3,2,1,0:T(2,128)(2,1)} %all-gather.2.cloned.1.call-done, bf16[]{:T(256)} %constant.126.clone.1), dimensions={0}, to_apply=%region_0.1 | reduce | flops 23592960 | bytes 53477376 | tf_op jit(solution)/shard_map/reduce_sum | solution.py:16
  354.8 7.9 %slice_convert_fusion = (f32[3,1,262144]{2,1,0:T(1,128)S(1)}, f32[3,1,262144]{2,1,0:T(1,128)S(1)}) fusion(bf16[3,2,262144]{2,1,0:T(2,128)(2,1)} %reduce_sum.30), kind=kLoop, calls=%fused_computation.71 | loop fusion | flops 1572864 | bytes 9437184 | tf_op jit(solution)/shard_map/convert_element_type | solution.py:74
  362.7 7.5 %copy_bitcast_fusion = (f32[3,262144]{1,0:T(4,128)}, f32[3,262144]{1,0:T(4,128)}) fusion(f32[3,1,262144]{2,1,0:T(1,128)S(1)} %get-tuple-element.234, f32[3,1,262144]{2,1,0:T(1,128)S(1)} %get-tuple-element.235), kind=kLoop, calls=%fused_computation.69 | loop fusion | bytes 12582912
  370.2 278.8 %while.15 = (s32[]{:T(128)}, f32[2]{0:T(128)S(1)}, f32[2]{0:T(128)S(1)}, s32[2]{0:T(128)S(1)}, f32[3,262144]{1,0:T(4,128)}, /*index=5*/bf16[2,2,262144]{2,1,0:T(...) while((s32[]{:T(128)}, f32[2]{0:T(128)S(1)}, ...), condition=%wide.region_5.6_spmd.clone.clone.clone, body=%wide.region_1.5_spmd.clone.clone.clone.sunk | while | flops 6514016256 | bytes 146276784 | solution.py:110
  382.6 16.5 %fusion.81 = (f32[262144]{0:T(1024)}, f32[262144]{0:T(1024)S(1)}, f32[1,1,262144]{2,1,0:T(1,128)}) fusion(bf16[2,2,262144]{2,1,0:T(2,128)(2,1)} %get-tuple-element.389, s32[]{:T(128)} %get-tuple-element.365, s32[]{:T(128)S(6)} %add.957), kind=kLoop, calls=%fused_computation.62.clone.1 | loop fusion | flops 1310720 | bytes 4194312 | tf_op jit(solution)/shard_map/while/body/eval_jaxpr/convert_element_type | solution.py:79
  401.3 2.0 copy.93
  404.9 42.3 %fusion.80 = (f32[3,262144]{1,0:T(4,128)S(1)}, f32[3,262144]{1,0:T(4,128)}) fusion(s32[3]{0:T(128)S(1)} %get-tuple-element.395, s32[262144]{0:T(1024)} %get-tuple-element.396, s32[3]{0:T(128)S(1)} %get-tuple-element.393, s32[262144]{0:T(1024)} %get-tuple-element.394), kind=kLoop, calls=%fused_computation.43.clone.1 | loop fusion | flops 29884416 | bytes 8388632 | tf_op jit(solution)/shard_map/sin | solution.py:35
  447.1 2.7 copy.84
  449.9 5.7 copy.85
  455.6 4.8 copy.86
  460.4 5.8 copy.87
  466.2 4.9 copy.88
  471.1 5.8 copy.89
  476.8 4.8 copy.91
  481.7 5.8 copy.92
  487.4 10.7 %select_convert_fusion.3 = (bf16[3,8,64,512]{2,3,1,0:T(8,128)(2,1)S(1)}, bf16[3,8,64,512]{2,3,1,0:T(8,128)(2,1)S(1)}) fusion(f32[3,8,64,512]{2,3,1,0:T(8,128)} %copy.85, f32[3,8,64,512]{2,3,1,0:T(8,128)} %copy.87, pred[8,64,512]{1,2,0:T(8,128)(4,1)S(1)} %add_compare_fusion.2, f32[3,8,64,512]{2,3,1,0:T(8,128)} %copy.89, f32[8,64,512]{1,2,0:T(8,128)S(1)} %copy.90, ...), kind=kLoop, calls=%fused_computation.22.clone.1 | loop fusion | flops 12582912 | bytes 18087936 | tf_op jit(solution)/shard_map/convert.5
  498.1 3.6 fusion.82
  501.8 4.1 fusion.83
  507.5 3.9 multiply_reduce_fusion.2
  512.3 1.5 select_reduce_fusion.2
  515.8 16.6 %fusion.81 = (f32[262144]{0:T(1024)}, f32[262144]{0:T(1024)S(1)}, f32[1,1,262144]{2,1,0:T(1,128)}) fusion(bf16[2,2,262144]{2,1,0:T(2,128)(2,1)} %get-tuple-element.389, s32[]{:T(128)} %get-tuple-element.365, s32[]{:T(128)S(6)} %add.957), kind=kLoop, calls=%fused_computation.62.clone.1 | loop fusion | flops 1310720 | bytes 4194312 | tf_op jit(solution)/shard_map/while/body/eval_jaxpr/convert_element_type | solution.py:79
  534.5 2.0 copy.93
  538.1 42.3 %fusion.80 = (f32[3,262144]{1,0:T(4,128)S(1)}, f32[3,262144]{1,0:T(4,128)}) fusion(s32[3]{0:T(128)S(1)} %get-tuple-element.395, s32[262144]{0:T(1024)} %get-tuple-element.396, s32[3]{0:T(128)S(1)} %get-tuple-element.393, s32[262144]{0:T(1024)} %get-tuple-element.394), kind=kLoop, calls=%fused_computation.43.clone.1 | loop fusion | flops 29884416 | bytes 8388632 | tf_op jit(solution)/shard_map/sin | solution.py:35
  580.4 2.7 copy.84
  583.1 5.7 copy.85
  588.8 4.8 copy.86
  593.6 5.8 copy.87
  599.4 4.9 copy.88
  604.3 5.8 copy.89
  610.0 4.8 copy.91
  614.9 5.8 copy.92
  620.7 10.7 %select_convert_fusion.3 = (bf16[3,8,64,512]{2,3,1,0:T(8,128)(2,1)S(1)}, bf16[3,8,64,512]{2,3,1,0:T(8,128)(2,1)S(1)}) fusion(f32[3,8,64,512]{2,3,1,0:T(8,128)} %copy.85, f32[3,8,64,512]{2,3,1,0:T(8,128)} %copy.87, pred[8,64,512]{1,2,0:T(8,128)(4,1)S(1)} %add_compare_fusion.2, f32[3,8,64,512]{2,3,1,0:T(8,128)} %copy.89, f32[8,64,512]{1,2,0:T(8,128)S(1)} %copy.90, ...), kind=kLoop, calls=%fused_computation.22.clone.1 | loop fusion | flops 12582912 | bytes 18087936 | tf_op jit(solution)/shard_map/convert.5
  631.4 3.6 fusion.82
  635.0 4.1 fusion.83
  640.7 3.9 multiply_reduce_fusion.2
  645.5 1.5 select_reduce_fusion.2
  (64 shorter events, 18.4 us)
Async XLA Ops:
  7.2 6.6 %copy-start = (bf16[32,2,16384]{2,1,0:T(2,128)(2,1)S(1)}, bf16[32,2,16384]{2,1,0:T(2,128)(2,1)}, u32[]{:S(2)}) copy-start(bf16[32,2,16384]{2,1,0:T(2,128)(2,1)} %param.9) | copy-start | bytes 6291460
  7.2 298.9 %all-gather.2.cloned.1.call-start = ((), (), s32[]{:S(2)}) async-start(), calls=%async_computation.1 | async-start | bytes 53477376 | tf_op jit(solution)/shard_map/all_gather | solution.py:16
  12.2 0.7 copy-start.7
  19.9 76.9 %all-to-all-start = ((bf16[16,2,2,16384]{3,2,1,0:T(2,128)(2,1)}), bf16[16,2,2,16384]{3,2,1,0:T(2,128)(2,1)}, u32[]{:S(2)}, u32[]{:S(2)}) async-start(bf16[16,2,2,16384]{3,2,1,0:T(2,128)(2,1)} %bitcast.88), calls=%async_computation | async-start | bytes 4194304 | tf_op jit(solution)/shard_map/all_to_all | solution.py:52
  46.5 1.6 copy-start.2
  46.5 2.2 copy-start.6
  487.4 10.7 %copy-start.5 = (bf16[8,1024,128]{2,1,0:T(8,128)(2,1)S(1)}, bf16[8,1024,128]{2,1,0:T(8,128)(2,1)}, u32[]{:S(2)}) copy-start(bf16[8,1024,128]{2,1,0:T(8,128)(2,1)} %get-tuple-element.391) | copy-start | bytes 6291460 | tf_op jit(solution)/shard_map/while
  505.9 1.6 copy-start.4
  507.5 4.9 copy-start.3
  620.6 10.7 %copy-start.5 = (bf16[8,1024,128]{2,1,0:T(8,128)(2,1)S(1)}, bf16[8,1024,128]{2,1,0:T(8,128)(2,1)}, u32[]{:S(2)}) copy-start(bf16[8,1024,128]{2,1,0:T(8,128)(2,1)} %get-tuple-element.391) | copy-start | bytes 6291460 | tf_op jit(solution)/shard_map/while
  639.1 1.6 copy-start.4
  640.7 4.9 copy-start.3
  649.0 0.5 copy-start.8
  649.0 0.5 copy-start.9
  649.0 1.6 copy-start.1
Sparse Core Ops, SparseCore 0:
  12.3 293.6 all-gather.1
